TPU v7x, 256 devices: a whole 4x4x8 slice. The times are simulated.
256 devices in a mesh: dp: 128 (over z, x_lo, y, core), tensor: 2 (over x_hi).
Axes of the slice: x: 4 (x_hi: 2, x_lo: 2; x = x_hi * 2 + x_lo), y: 4, z: 8, core: 2. Of those that a mesh axis runs over, the one named last changes fastest.
Arguments:
- looked: bfloat16 [8192, 16384], P(('dp', 'tensor')), may hold values from -6 to 6
- column_owner: int32 [8192], replicated, may hold values from 0 to 8191, each once
- v_proj: bfloat16 [384, 8192], P(None, 'tensor'), may hold values from -0.0625 to 0.0625
- u_proj: bfloat16 [384, 8192], P(None, 'tensor'), may hold values from -0.3125 to 0.3125
- bias: float32 [8192], P('tensor'), may hold values from -3 to 3
- upstream: bfloat16 [8192, 16384], P('tensor', 'dp'), may hold values from -6 to 6
Outputs:
- d_looked: bfloat16 [8192, 16384], P(('dp', 'tensor'))
- grad_u: float32 [384, 8192], P('dp', 'tensor')
- grad_v: float32 [384, 8192], P('dp', 'tensor')
- grad_bias: float32 [8192], P('tensor')
Inputs may be any that keep to these rules, and one draw needn't show every extreme that they name: A permutation of the 8192 feature columns: wire row r carries column column_owner[r].
All inputs are finite; a program needn't handle non-finite values.
Results may differ from a plain program's by a relative error of at most 0.0049.
Values may be sent and summed in bfloat16 or wider, within the bound.
No kernel may reach another device: no remote copies, remote signals or barrier semaphores. Data moves between devices by JAX's collectives and lax.ppermute only.
A program may use at most 128 MiB of HBM per device.

v0:
```python
import math
import jax
import jax.numpy as jnp
from jax import lax
from jax.sharding import PartitionSpec as P


def contract_last(left, right):
    return lax.dot_general(
        left, right, (((1,), (1,)), ((), ())), preferred_element_type=jnp.float32
    )


def contract_first(left, right):
    return lax.dot_general(
        left, right, (((0,), (0,)), ((), ())), preferred_element_type=jnp.float32
    )


def rank_cotangent(u_proj, scaled16):
    dh_part = jnp.dot(u_proj, scaled16, preferred_element_type=jnp.float32)
    return lax.psum(dh_part, "tensor").astype(jnp.bfloat16)


def per_device(looked, column_owner, v_proj, u_proj, bias, upstream):
    dp_count = lax.axis_size("dp")
    pair_count = lax.axis_size("tensor")
    pair_index = lax.axis_index("tensor")
    block_rows = looked.shape[0]
    half_width = v_proj.shape[1]
    full_width = half_width * pair_count
    local_samples = upstream.shape[1]
    norm = 1.0 / math.sqrt(local_samples * dp_count)
    wire_ids = jnp.arange(full_width, dtype=jnp.int32)
    inverse = jnp.zeros((full_width,), jnp.int32).at[column_owner].set(wire_ids)
    mine_wire = lax.dynamic_slice_in_dim(inverse, pair_index * half_width, half_width)
    arrived = lax.all_to_all(looked, "dp", split_axis=1, concat_axis=0, tiled=True)
    paired = lax.all_gather(arrived, "tensor", axis=0, tiled=True)
    block_ids = mine_wire // block_rows
    within = mine_wire % block_rows
    gather_rows = (
        block_ids % pair_count * (dp_count * block_rows)
        + block_ids // pair_count * block_rows
        + within
    )
    x_zero = jnp.take(paired, gather_rows, axis=0)
    h_part = jnp.dot(v_proj, x_zero, preferred_element_type=jnp.float32)
    hrank = lax.psum(h_part, "tensor").astype(jnp.bfloat16)
    mix = contract_first(u_proj, hrank) + bias[:, None]
    cotan = upstream.astype(jnp.float32)
    scaled = cotan * x_zero.astype(jnp.float32)
    scaled16 = scaled.astype(jnp.bfloat16)
    grad_bias = lax.psum(jnp.sum(scaled, axis=1), "dp") * norm
    dhrank = rank_cotangent(u_proj, scaled16)
    first = contract_last(hrank, scaled16)
    second = contract_last(dhrank, x_zero)
    joined_grads = (
        lax.psum_scatter(
            jnp.concatenate([first, second], axis=1), "dp", scatter_dimension=0, tiled=True
        )
        * norm
    )
    grad_u = joined_grads[:, :half_width]
    grad_v = joined_grads[:, half_width:]
    dx_zero = (cotan * (mix + 1.0) + contract_first(v_proj, dhrank)).astype(jnp.bfloat16)
    dx_full = lax.all_gather(dx_zero, "tensor", axis=0, tiled=True)
    send_wire = (
        (jnp.arange(dp_count, dtype=jnp.int32)[:, None] * pair_count + pair_index) * block_rows
        + jnp.arange(block_rows, dtype=jnp.int32)[None, :]
    ).reshape(-1)
    send_cols = jnp.take(column_owner, send_wire, axis=0)
    outgoing = jnp.take(dx_full, send_cols, axis=0)
    d_looked = lax.all_to_all(outgoing, "dp", split_axis=0, concat_axis=1, tiled=True)
    return (d_looked, grad_u, grad_v, grad_bias)


def solution(mesh):
    in_specs = (
        P(("dp", "tensor"), None),
        P(),
        P(None, "tensor"),
        P(None, "tensor"),
        P("tensor"),
        P("tensor", "dp"),
    )
    out_specs = (P(("dp", "tensor"), None), P("dp", "tensor"), P("dp", "tensor"), P("tensor"))
    return jax.shard_map(
        per_device, mesh=mesh, in_specs=in_specs, out_specs=out_specs, check_vma=False
    )
```

profile of v0, /device:TPU:4, one launch (start us, length us, event | category | flops | bytes accessed | tf_op | source)
XLA Modules:
  0.0 1323.6 jit_solution(17877898504607642298)
XLA Ops:
  7.2 1.6 copy_bitcast_fusion.1
  8.8 43.1 %all_to_all.38 = bf16[32,128,128]{2,0,1:T(8,128)(2,1)} all-to-all(bf16[32,128,128]{2,0,1:T(8,128)(2,1)S(1)} %copy_bitcast_fusion.1), channel_id=1, replica_groups=mesh['dp'=128,'tensor'=2] {'dp'}, dimensions={1} | all-to-all | bytes 2097152 | tf_op jit(solution)/shard_map/all_to_all | solution.py:37
  52.0 2.3 copy.20
  54.3 30.5 %scatter_custom_fusion = s32[8192]{0:T(1024)S(1)} fusion(s32[8192]{0:T(1024)S(1)} %compare_select_fusion.1, s32[8192]{0:T(1024)S(1)} %iota.12, s32[]{:T(128)} %constant.77.clone.1), kind=kCustom, calls=%fused_computation.54 | custom fusion | bytes 32772 | tf_op jit(solution)/shard_map/scatter | solution.py:35
  84.9 0.5 all-gather.3.cloned.1.call-done
  85.3 16.1 %gather_fusion.1 = bf16[4096,128]{1,0:T(8,128)(2,1)} fusion(bf16[8192,128]{1,0:T(8,128)(2,1)} %all-gather.3.cloned.1.call-done, s32[4096]{0:T(1024)S(1)} %broadcast_clamp_fusion.1), kind=kCustom, calls=%fused_computation.clone | custom fusion | bytes 2113536 | tf_op jit(solution)/shard_map/jit(_take)/gather | solution.py:46
  101.4 2.3 copy.22
  103.7 3.4 convolution_bitcast_fusion.1
  107.2 1.7 convolution_bitcast_fusion.2
  108.9 17.8 %all-reduce.6 = (bf16[384,128]{0,1:T(8,128)(2,1)S(1)}, bf16[384,128]{0,1:T(8,128)(2,1)S(1)}) all-reduce(f32[384,128]{0,1:T(8,128)} %convolution_bitcast_fusion.2, f32[384,128]{0,1:T(8,128)} %convolution_bitcast_fusion.1), channel_id=1, replica_groups=mesh['dp'=128,'tensor'=2] {'tensor'}, use_global_device_ids=true, to_apply=%region_1.3 | all-reduce | flops 98304 | bytes 589824 | tf_op jit(solution)/shard_map/psum | solution.py:48
  126.8 2.1 fusion.3
  128.9 0.1 copy-done.6
  129.0 1.7 fusion.4
  130.7 0.2 all-reduce.5.cloned.1.call-start
  131.0 5.0 fusion.7
  135.9 3.6 fusion.10
  139.5 10.8 pad_maximum_fusion
  150.4 0.1 iota_add_fusion
  150.5 0.1 add.144
  150.7 23.0 %gather_fusion = s32[4096]{0:T(1024)S(1)} fusion(s32[8192]{0:T(1024)S(1)} %copy-done.1, s32[4096]{0:T(1024)S(1)} %broadcast_clamp_fusion.2), kind=kCustom, calls=%fused_computation.2 | custom fusion | bytes 49152 | tf_op jit(solution)/shard_map/jit(_take)/gather | solution.py:71
  173.8 4.1 copy.23
  177.9 16.1 %gather_fusion.2 = bf16[4096,128]{1,0:T(8,128)(2,1)} fusion(bf16[8192,128]{1,0:T(8,128)(2,1)} %copy.23, s32[4096]{0:T(1024)S(1)} %broadcast_clamp_fusion), kind=kCustom, calls=%fused_computation.1.clone | custom fusion | bytes 2113536 | tf_op jit(solution)/shard_map/jit(_take)/gather | solution.py:72
  193.9 4.2 broadcast_select_fusion
  198.2 12.8 all-to-all-start.1
  211.0 0.6 dynamic-slice
  212.3 1.9 fusion.5
  214.2 564.8 %psum.23 = f32[4096]{0:T(1024)S(1)} all-reduce(f32[4096]{0:T(1024)S(1)} %fusion.5), channel_id=1, replica_groups=mesh['dp'=128,'tensor'=2] {'dp'}, use_global_device_ids=true, to_apply=%region_5.7 | all-reduce | flops 4096 | bytes 32768 | tf_op jit(solution)/shard_map/psum | solution.py:53
  779.0 0.6 broadcast_multiply_fusion
  779.7 2.3 copy_bitcast_fusion
  781.9 533.3 %all-reduce.5.cloned.1.call-done = f32[384,8192]{1,0:T(8,128)} async-done(((f32[384,8192]{1,0:T(8,128)}), f32[384,8192]{1,0:T(8,128)}) %all-reduce.5.cloned.1.call-update) | async-done | bytes 12582928
  1315.3 1.1 dynamic-slice_multiply_fusion
  1316.3 0.7 fusion.33
  (34 shorter events, 0.4 us)
Async XLA Ops:
  7.2 96.6 %copy-start = (bf16[384,4096]{1,0:T(8,128)(2,1)S(1)}, bf16[384,4096]{1,0:T(8,128)(2,1)}, u32[]{:S(2)}) copy-start(bf16[384,4096]{1,0:T(8,128)(2,1)} %param.11) | copy-start | bytes 9437188
  7.2 78.2 %all-gather.3.cloned.1.call-start = ((), (), s32[]{:S(2)}) async-start(), calls=%async_computation.2 | async-start | bytes 3145728 | tf_op jit(solution)/shard_map/all_gather | solution.py:38
  8.8 45.5 %copy-start.1 = (s32[8192]{0:T(1024)S(1)}, s32[8192]{0:T(1024)}, u32[]{:S(2)}) copy-start(s32[8192]{0:T(1024)} %param.9) | copy-start | bytes 98308
  52.0 121.8 %all-gather.5.cloned.1.call-start = ((), (), s32[]{:S(2)}) async-start(), calls=%async_computation.3 | async-start | bytes 3145728 | tf_op jit(solution)/shard_map/all_gather | solution.py:66
  103.7 3.4 copy-start.3
  103.7 3.4 copy-start.5
  107.2 19.6 %copy-start.7 = (f32[4096]{0:T(1024)S(1)}, f32[4096]{0:T(1024)}, u32[]{:S(2)}) copy-start(f32[4096]{0:T(1024)} %param.12) | copy-start | bytes 49156
  126.7 2.2 copy-start.6
  130.7 1184.6 %all-reduce.5.cloned.1.call-start = ((), (), s32[]{:S(2)}) async-start(), calls=%async_computation.4 | async-start | bytes 25165824
  130.9 5.0 copy-start.2
  130.9 5.0 copy-start.4
  193.9 17.1 %copy-start.8 = (u32[256]{0:T(256)S(1)}, u32[256]{0:T(256)}, u32[]{:S(2)}) copy-start(u32[256]{0:T(256)} %constant.95) | copy-start | bytes 3076
  198.2 581.5 %all-to-all-start.1 = ((bf16[128,32,128]{2,1,0:T(8,128)(2,1)}), bf16[128,32,128]{2,1,0:T(8,128)(2,1)}, u32[]{:S(2)}, u32[]{:S(2)}) async-start(bf16[128,32,128]{2,1,0:T(8,128)(2,1)} %bitcast.41), calls=%async_computation.1 | async-start | bytes 2097152 | tf_op jit(solution)/shard_map/all_to_all | solution.py:73
Sparse Core Ops, SparseCore 0:
  52.1 33.2 all-gather.2
  130.8 38.3 all-gather.4
  171.8 1143.4 all-reduce.4
where the time goes:
time: 1320 us
  blocking collectives  626 us (47%)
  waiting for transfers between devices  534 us (40%)
  local copies, waits for them, and re-layouts  99.7 us (8%)
  other arithmetic  18.8 us (1%)
  matrix products  17.6 us (1%)
  between operations  14.6 us (1%)
    psum x1, blocking collectives, per_device(): grad_bias = lax.psum(jnp.sum(scaled, axis=1), 'dp') * norm  565 us
    unnamed x4, waiting for transfers between devices  533 us
    all_to_all x1, blocking collectives, per_device(): lax.all_to_all(looked, 'dp', split_axis=1, concat_axis=0, tiled=True)  43.1 us
    scatter x1, local copies, waits for them, and re-layouts, per_device(): inverse = jnp.zeros((full_width,), jnp.int32).at[column_owner].set(wire_ids)  30.5 us
  transfers between devices with their start and end apart: 4, of which 2 were waited for; matrix products, arithmetic and copies ran while one was open for 8% of the time, Pallas kernels for 0%

commit v1 on v0

--- a/solution.py
+++ b/solution.py
@@ -50,7 +50,7 @@
     cotan = upstream.astype(jnp.float32)
     scaled = cotan * x_zero.astype(jnp.float32)
     scaled16 = scaled.astype(jnp.bfloat16)
-    grad_bias = lax.psum(jnp.sum(scaled, axis=1), "dp") * norm
+    grad_bias = jnp.sum(lax.all_gather(jnp.sum(scaled, axis=1), "dp"), axis=0) * norm
     dhrank = rank_cotangent(u_proj, scaled16)
     first = contract_last(hrank, scaled16)
     second = contract_last(dhrank, x_zero)

time: 1320 us -> 1530 us (1.16)
  waiting for transfers between devices: 534 us -> 1310 us
  blocking collectives: 626 us -> 60.9 us
    unnamed x4 -> x5, waiting for transfers between devices: 533 us -> 1130 us
    psum x1 -> x0, blocking collectives: 565 us -> none  [per_device(): grad_bias = lax.psum(jnp.sum(scaled, axis=1), 'dp') * norm]
    all_gather x0 -> x1, waiting for transfers between devices: none -> 184 us  [per_device(): lax.all_gather(jnp.sum(scaled, axis=1), 'dp')]
  transfers between devices with their start and end apart: 4 -> 5, of which waited for: 2 -> 3; matrix products, arithmetic and copies ran while one was open for 8% -> 7% of each run, Pallas kernels for 0% -> 0%
where the time goes in v1:
time: 1530 us
  waiting for transfers between devices  1310 us (86%)
  local copies, waits for them, and re-layouts  97.8 us (6%)
  blocking collectives  60.9 us (4%)
  other arithmetic  18.1 us (1%)
  matrix products  16.3 us (1%)
    unnamed x5, waiting for transfers between devices  1130 us
    all_gather x1, waiting for transfers between devices, per_device(): lax.all_gather(jnp.sum(scaled, axis=1), 'dp')  184 us
    all_to_all x1, blocking collectives, per_device(): lax.all_to_all(looked, 'dp', split_axis=1, concat_axis=0, tiled=True)  43.1 us
  transfers between devices with their start and end apart: 5, of which 3 were waited for; matrix products, arithmetic and copies ran while one was open for 7% of the time, Pallas kernels for 0%

profile of v1, /device:TPU:4, one launch (start us, length us, event | category | flops | bytes accessed | tf_op | source)
XLA Modules:
  0.0 1532.6 jit_solution(14096320162784187307)
XLA Ops:
  7.2 1.6 copy_bitcast_fusion.1
  8.8 43.1 %all_to_all.38 = bf16[32,128,128]{2,0,1:T(8,128)(2,1)} all-to-all(bf16[32,128,128]{2,0,1:T(8,128)(2,1)S(1)} %copy_bitcast_fusion.1), channel_id=1, replica_groups=mesh['dp'=128,'tensor'=2] {'dp'}, dimensions={1} | all-to-all | bytes 2097152 | tf_op jit(solution)/shard_map/all_to_all | solution.py:37
  52.0 2.3 copy.25
  54.3 30.5 %scatter_custom_fusion = s32[8192]{0:T(1024)S(1)} fusion(s32[8192]{0:T(1024)S(1)} %compare_select_fusion.1, s32[8192]{0:T(1024)S(1)} %iota.12, s32[]{:T(128)} %constant.77.clone.1), kind=kCustom, calls=%fused_computation.54 | custom fusion | bytes 32772 | tf_op jit(solution)/shard_map/scatter | solution.py:35
  84.9 0.5 all-gather.5.cloned.1.call-done
  85.3 16.1 %gather_fusion.1 = bf16[4096,128]{1,0:T(8,128)(2,1)} fusion(bf16[8192,128]{1,0:T(8,128)(2,1)} %all-gather.5.cloned.1.call-done, s32[4096]{0:T(1024)S(1)} %broadcast_clamp_fusion.1), kind=kCustom, calls=%fused_computation.clone | custom fusion | bytes 2113536 | tf_op jit(solution)/shard_map/jit(_take)/gather | solution.py:46
  101.4 2.3 copy.27
  103.7 3.4 convolution_bitcast_fusion.1
  107.1 1.8 convolution_bitcast_fusion.2
  108.9 17.8 %all-reduce.6 = (bf16[384,128]{0,1:T(8,128)(2,1)S(1)}, bf16[384,128]{0,1:T(8,128)(2,1)S(1)}) all-reduce(f32[384,128]{0,1:T(8,128)} %convolution_bitcast_fusion.2, f32[384,128]{0,1:T(8,128)} %convolution_bitcast_fusion.1), channel_id=1, replica_groups=mesh['dp'=128,'tensor'=2] {'tensor'}, use_global_device_ids=true, to_apply=%region_1.3 | all-reduce | flops 98304 | bytes 589824 | tf_op jit(solution)/shard_map/psum | solution.py:48
  126.7 2.1 fusion.3
  128.9 1.8 fusion.4
  130.8 1.0 fusion.5
  131.9 0.2 all-reduce.5.cloned.1.call-start
  132.1 3.6 fusion.7
  135.7 3.6 fusion.10
  139.3 10.7 pad_maximum_fusion
  150.1 0.1 add.142
  150.3 23.0 %gather_fusion = s32[4096]{0:T(1024)S(1)} fusion(s32[8192]{0:T(1024)S(1)} %copy-done.2, s32[4096]{0:T(1024)S(1)} %broadcast_clamp_fusion.2), kind=kCustom, calls=%fused_computation.2 | custom fusion | bytes 49152 | tf_op jit(solution)/shard_map/jit(_take)/gather | solution.py:71
  173.4 3.2 copy.28
  176.6 12.1 gather_fusion.2
  188.8 2.9 broadcast_select_fusion
  191.7 12.8 all-to-all-start.1
  204.5 0.6 dynamic-slice
  205.8 183.5 %all-gather.9.cloned.1.call-done = f32[524288]{0:T(1024)} async-done(((f32[4096]{0:T(1024)}), f32[524288]{0:T(1024)}) %all-gather.9.cloned.1.call-update) | async-done | bytes 2097168 | tf_op jit(solution)/shard_map/all_gather | solution.py:53
  389.3 2.9 reshape.100
  392.2 1.7 reduce_sum.19
  393.9 0.6 broadcast_multiply_fusion
  394.5 2.3 copy_bitcast_fusion
  396.8 1127.5 %all-reduce.5.cloned.1.call-done = f32[384,8192]{1,0:T(8,128)} async-done(((f32[384,8192]{1,0:T(8,128)}), f32[384,8192]{1,0:T(8,128)}) %all-reduce.5.cloned.1.call-update) | async-done | bytes 12582928
  1524.3 1.1 dynamic-slice_multiply_fusion
  1525.3 0.7 fusion.33
  (40 shorter events, 0.6 us)
Async XLA Ops:
  7.2 96.5 %copy-start = (bf16[384,4096]{1,0:T(8,128)(2,1)S(1)}, bf16[384,4096]{1,0:T(8,128)(2,1)}, u32[]{:S(2)}) copy-start(bf16[384,4096]{1,0:T(8,128)(2,1)} %param.11) | copy-start | bytes 9437188
  7.2 78.1 %all-gather.5.cloned.1.call-start = ((), (), s32[]{:S(2)}) async-start(), calls=%async_computation.2 | async-start | bytes 3145728 | tf_op jit(solution)/shard_map/all_gather | solution.py:38
  51.9 2.4 copy-start.2
  52.0 121.4 %all-gather.7.cloned.1.call-start = ((), (), s32[]{:S(2)}) async-start(), calls=%async_computation.3 | async-start | bytes 3145728 | tf_op jit(solution)/shard_map/all_gather | solution.py:66
  103.7 3.4 copy-start.4
  103.7 3.4 copy-start.6
  107.1 19.6 %copy-start.8 = (f32[4096]{0:T(1024)S(1)}, f32[4096]{0:T(1024)}, u32[]{:S(2)}) copy-start(f32[4096]{0:T(1024)} %param.12) | copy-start | bytes 49156
  126.7 2.2 copy-start.7
  128.9 1.9 copy-start.3
  128.9 1.9 copy-start.5
  130.8 258.5 %all-gather.9.cloned.1.call-start = ((), (), s32[]{:S(2)}) async-start(), calls=%async_computation.4 | async-start | bytes 2113536 | tf_op jit(solution)/shard_map/all_gather | solution.py:53
  131.9 1392.4 %all-reduce.5.cloned.1.call-start = ((), (), s32[]{:S(2)}) async-start(), calls=%async_computation.5 | async-start | bytes 25165824
  188.8 15.7 %copy-start.9 = (u32[256]{0:T(256)S(1)}, u32[256]{0:T(256)}, u32[]{:S(2)}) copy-start(u32[256]{0:T(256)} %constant.95) | copy-start | bytes 3076
  191.7 202.8 %all-to-all-start.1 = ((bf16[128,32,128]{2,1,0:T(8,128)(2,1)}), bf16[128,32,128]{2,1,0:T(8,128)(2,1)}, u32[]{:S(2)}, u32[]{:S(2)}) async-start(bf16[128,32,128]{2,1,0:T(8,128)(2,1)} %bitcast.7), calls=%async_computation.1 | async-start | bytes 2097152 | tf_op jit(solution)/shard_map/all_to_all | solution.py:73
  389.3 1136.7 %copy-start.1 = (bf16[384,4096]{1,0:T(8,128)(2,1)S(1)}, bf16[384,4096]{1,0:T(8,128)(2,1)}, u32[]{:S(2)}) copy-start(bf16[384,4096]{1,0:T(8,128)(2,1)} %param.11) | copy-start | bytes 9437188
Sparse Core Ops, SparseCore 0:
  52.1 33.2 all-gather.4
  130.9 38.3 all-gather.6
  171.7 217.5 all-gather.8
  391.8 1132.4 all-reduce.4
